TPU v7x, 32 devices: a whole 2x2x4 slice. The times are simulated.
32 devices in a mesh: rep: 8 (over y, x, core), grp: 4 (over z).
Axes of the slice: x: 2, y: 2, z: 4, core: 2. Of those that a mesh axis runs over, the one named last changes fastest.
Arguments:
- images: bfloat16 [32, 577, 1024], P(('rep', 'grp')), may hold values from -6 to 6
- cotangent: bfloat16 [32, 577, 1024], P(('rep', 'grp')), may hold values from -6 to 6
- ln1_gain: bfloat16 [1024], P('grp'), may hold values from 0.5 to 1.5
- ln1_shift: bfloat16 [1024], P('grp'), may hold values from -3 to 3
- qkv_weight: bfloat16 [1024, 3072], P('grp'), may hold values from -1 to 1
- qv_bias: bfloat16 [2048], P('grp'), may hold values from -3 to 3
- out_weight: bfloat16 [1024, 1024], P('grp'), may hold values from -1.5 to 1.5
- out_bias: bfloat16 [1024], P('grp'), may hold values from -3 to 3
- ln2_gain: bfloat16 [1024], P('grp'), may hold values from 0.5 to 1.5
- ln2_shift: bfloat16 [1024], P('grp'), may hold values from -3 to 3
- fc1_weight: bfloat16 [1024, 4096], P('grp'), may hold values from -0.1875 to 0.1875
- fc1_bias: bfloat16 [4096], P('grp'), may hold values from -3 to 3
- fc2_weight: bfloat16 [4096, 1024], P('grp'), may hold values from -0.09375 to 0.09375
- fc2_bias: bfloat16 [1024], P('grp'), may hold values from -3 to 3
Outputs:
- outputs: bfloat16 [32, 577, 1024], P(('rep', 'grp'))
- input_grad: bfloat16 [32, 577, 1024], P(('rep', 'grp'))
- grad_ln1_gain: float32 [1024], P('grp')
- grad_ln1_shift: float32 [1024], P('grp')
- grad_qkv_weight: float32 [1024, 3072], P('grp')
- grad_qv_bias: float32 [2048], P('grp')
- grad_out_weight: float32 [1024, 1024], P('grp')
- grad_out_bias: float32 [1024], P('grp')
- grad_ln2_gain: float32 [1024], P('grp')
- grad_ln2_shift: float32 [1024], P('grp')
- grad_fc1_weight: float32 [1024, 4096], P('grp')
- grad_fc1_bias: float32 [4096], P('grp')
- grad_fc2_weight: float32 [4096, 1024], P('grp')
- grad_fc2_bias: float32 [1024], P('grp')
All inputs are finite; a program needn't handle non-finite values.
Results may differ from a plain program's by a relative error of at most 0.012.
Values may be sent and summed in bfloat16 or wider, within the bound.
No kernel may reach another device: no remote copies, remote signals or barrier semaphores. Data moves between devices by JAX's collectives and lax.ppermute only.
A program may use at most 256 MiB of HBM per device.

v0:
```python
import math
import jax
import jax.numpy as jnp
from jax import lax
from jax.sharding import PartitionSpec as P

H = 16
HD = 64
root_half = 0.7071067811865476
inv_root_tau = 0.3989422804014327


def norm_forward(values, gain_vec, shift_vec):
    row_mean = jnp.mean(values, axis=-1, keepdims=True)
    centred = values - row_mean
    inv_std = lax.rsqrt(jnp.mean(centred * centred, axis=-1, keepdims=True) + 1e-06)
    normed = centred * inv_std
    return (normed * gain_vec + shift_vec, normed, inv_std)


def norm_backward(grad_out, normed, inv_std, gain_vec):
    grad_hat = grad_out * gain_vec
    grad_in = inv_std * (
        grad_hat
        - jnp.mean(grad_hat, axis=-1, keepdims=True)
        - normed * jnp.mean(grad_hat * normed, axis=-1, keepdims=True)
    )
    return (grad_in, jnp.sum(grad_out * normed, axis=0), jnp.sum(grad_out, axis=0))


def split_heads(matrix):
    return matrix.reshape(matrix.shape[0], H, HD).transpose(1, 0, 2)


def join_heads(tensor):
    return tensor.transpose(1, 0, 2).reshape(tensor.shape[1], H * HD)


def grouped(tensor):
    group_size = math.gcd(H, 4)
    return tensor.reshape((H // group_size, group_size) + tensor.shape[1:])


def ungrouped(tensor):
    return tensor.reshape((H,) + tensor.shape[2:])


def head_scores(query_group, key_group):
    return jnp.einsum("hqd,hkd->hqk", query_group, key_group, preferred_element_type=jnp.float32)


def attend_group(group):
    query_group, key_group, value_group = group
    scores = head_scores(query_group, key_group)
    row_max = jnp.max(scores, axis=-1, keepdims=True)
    log_total = row_max + jnp.log(jnp.sum(jnp.exp(scores - row_max), axis=-1, keepdims=True))
    probs = jnp.exp(scores - log_total).astype(jnp.bfloat16)
    mixed = jnp.einsum("hqk,hkd->hqd", probs, value_group, preferred_element_type=jnp.float32)
    return (mixed, log_total)


def attend_back(group):
    query_group, key_group, value_group, log_total, grad_mixed = group
    probs_exact = jnp.exp(head_scores(query_group, key_group) - log_total)
    grad_probs = jnp.einsum(
        "hqd,hkd->hqk", grad_mixed, value_group, preferred_element_type=jnp.float32
    )
    row_dot = jnp.sum(probs_exact * grad_probs, axis=-1, keepdims=True)
    grad_scores = (probs_exact * (grad_probs - row_dot)).astype(jnp.bfloat16)
    grad_query = (
        jnp.einsum("hqk,hkd->hqd", grad_scores, key_group, preferred_element_type=jnp.float32)
        * 0.125
    )
    grad_key = jnp.einsum(
        "hqk,hqd->hkd", grad_scores, query_group, preferred_element_type=jnp.float32
    )
    grad_value = jnp.einsum(
        "hqk,hqd->hkd",
        probs_exact.astype(jnp.bfloat16),
        grad_mixed,
        preferred_element_type=jnp.float32,
    )
    return (grad_query, grad_key, grad_value)


def forward_image(image, params):
    (
        gain_first,
        shift_first,
        attn_in,
        bias_pair,
        attn_out,
        bias_attn,
        gain_second,
        shift_second,
        mlp_up,
        bias_up,
        mlp_down,
        bias_down,
    ) = params
    model_width = attn_out.shape[0]
    incoming = image.astype(jnp.float32)
    normed_f, normed_one, inv_std_one = norm_forward(
        incoming, gain_first.astype(jnp.float32), shift_first.astype(jnp.float32)
    )
    normed_in = normed_f.astype(jnp.bfloat16)
    projected = jnp.dot(normed_in, attn_in, preferred_element_type=jnp.float32)
    bias_float = bias_pair.astype(jnp.float32)
    query_heads = split_heads(
        ((projected[:, :model_width] + bias_float[:model_width]) * 0.125).astype(jnp.bfloat16)
    )
    key_heads = split_heads(projected[:, model_width : 2 * model_width].astype(jnp.bfloat16))
    value_heads = split_heads(
        (projected[:, 2 * model_width :] + bias_float[model_width:]).astype(jnp.bfloat16)
    )
    mixed, log_total = lax.map(
        attend_group, (grouped(query_heads), grouped(key_heads), grouped(value_heads))
    )
    attended = join_heads(ungrouped(mixed)).astype(jnp.bfloat16)
    residual = (
        incoming
        + jnp.dot(attended, attn_out, preferred_element_type=jnp.float32)
        + bias_attn.astype(jnp.float32)
    )
    mid_f, normed_two, inv_std_two = norm_forward(
        residual, gain_second.astype(jnp.float32), shift_second.astype(jnp.float32)
    )
    normed_mid = mid_f.astype(jnp.bfloat16)
    pre_act = jnp.dot(normed_mid, mlp_up, preferred_element_type=jnp.float32) + bias_up.astype(
        jnp.float32
    )
    normal_cdf = 0.5 * (1.0 + lax.erf(pre_act * root_half))
    activated = (pre_act * normal_cdf).astype(jnp.bfloat16)
    block_out = (
        residual
        + jnp.dot(activated, mlp_down, preferred_element_type=jnp.float32)
        + bias_down.astype(jnp.float32)
    ).astype(jnp.bfloat16)
    stored = (
        normed_in,
        normed_one,
        inv_std_one,
        query_heads,
        key_heads,
        value_heads,
        ungrouped(log_total),
        attended,
        normed_mid,
        normed_two,
        inv_std_two,
        pre_act,
        normal_cdf,
        activated,
    )
    return (block_out, stored)


def backward_image(grad_block, stored, params):
    (
        gain_first,
        shift_first,
        attn_in,
        bias_pair,
        attn_out,
        bias_attn,
        gain_second,
        shift_second,
        mlp_up,
        bias_up,
        mlp_down,
        bias_down,
    ) = params
    (
        normed_in,
        normed_one,
        inv_std_one,
        query_heads,
        key_heads,
        value_heads,
        log_total,
        attended,
        normed_mid,
        normed_two,
        inv_std_two,
        pre_act,
        normal_cdf,
        activated,
    ) = stored
    grad_top = grad_block.astype(jnp.float32)
    grad_down = jnp.dot(activated.T, grad_block, preferred_element_type=jnp.float32)
    grad_bias_down = jnp.sum(grad_top, axis=0)
    grad_hidden = jnp.dot(grad_block, mlp_down.T, preferred_element_type=jnp.float32)
    density = jnp.exp(-0.5 * pre_act * pre_act) * inv_root_tau
    grad_pre = grad_hidden * (normal_cdf + pre_act * density)
    grad_pre_b = grad_pre.astype(jnp.bfloat16)
    grad_up = jnp.dot(normed_mid.T, grad_pre_b, preferred_element_type=jnp.float32)
    grad_bias_up = jnp.sum(grad_pre, axis=0)
    grad_mid = jnp.dot(grad_pre_b, mlp_up.T, preferred_element_type=jnp.float32)
    grad_norm_mid, grad_gain_second, grad_shift_second = norm_backward(
        grad_mid, normed_two, inv_std_two, gain_second.astype(jnp.float32)
    )
    grad_residual = grad_top + grad_norm_mid
    grad_bias_attn = jnp.sum(grad_residual, axis=0)
    grad_res_b = grad_residual.astype(jnp.bfloat16)
    grad_attn_out = jnp.dot(attended.T, grad_res_b, preferred_element_type=jnp.float32)
    grad_attended = split_heads(
        jnp.dot(grad_res_b, attn_out.T, preferred_element_type=jnp.float32).astype(jnp.bfloat16)
    )
    grad_query, grad_key, grad_value = lax.map(
        attend_back,
        (
            grouped(query_heads),
            grouped(key_heads),
            grouped(value_heads),
            grouped(log_total),
            grouped(grad_attended),
        ),
    )
    grad_query = join_heads(ungrouped(grad_query))
    grad_key = join_heads(ungrouped(grad_key))
    grad_value = join_heads(ungrouped(grad_value))
    grad_projected = jnp.concatenate([grad_query, grad_key, grad_value], axis=1)
    grad_bias_pair = jnp.concatenate([jnp.sum(grad_query, axis=0), jnp.sum(grad_value, axis=0)])
    grad_proj_b = grad_projected.astype(jnp.bfloat16)
    grad_attn_in = jnp.dot(normed_in.T, grad_proj_b, preferred_element_type=jnp.float32)
    grad_in_norm = jnp.dot(grad_proj_b, attn_in.T, preferred_element_type=jnp.float32)
    grad_norm_in, grad_gain_first, grad_shift_first = norm_backward(
        grad_in_norm, normed_one, inv_std_one, gain_first.astype(jnp.float32)
    )
    input_grad = (grad_residual + grad_norm_in).astype(jnp.bfloat16)
    grads = (
        grad_gain_first,
        grad_shift_first,
        grad_attn_in,
        grad_bias_pair,
        grad_attn_out,
        grad_bias_attn,
        grad_gain_second,
        grad_shift_second,
        grad_up,
        grad_bias_up,
        grad_down,
        grad_bias_down,
    )
    return (input_grad, grads)


def on_device(
    images,
    cotangent,
    ln1_gain,
    ln1_shift,
    qkv_weight,
    qv_bias,
    out_weight,
    out_bias,
    ln2_gain,
    ln2_shift,
    fc1_weight,
    fc1_bias,
    fc2_weight,
    fc2_bias,
):
    gathered = (
        lax.all_gather(ln1_gain, "grp", axis=0, tiled=True),
        lax.all_gather(ln1_shift, "grp", axis=0, tiled=True),
        lax.all_gather(qkv_weight, "grp", axis=0, tiled=True),
        lax.all_gather(qv_bias, "grp", axis=0, tiled=True),
        lax.all_gather(out_weight, "grp", axis=0, tiled=True),
        lax.all_gather(out_bias, "grp", axis=0, tiled=True),
        lax.all_gather(ln2_gain, "grp", axis=0, tiled=True),
        lax.all_gather(ln2_shift, "grp", axis=0, tiled=True),
        lax.all_gather(fc1_weight, "grp", axis=0, tiled=True),
        lax.all_gather(fc1_bias, "grp", axis=0, tiled=True),
        lax.all_gather(fc2_weight, "grp", axis=0, tiled=True),
        lax.all_gather(fc2_bias, "grp", axis=0, tiled=True),
    )
    position = 0
    block_out, stored = forward_image(images[position], gathered)
    block_outs = [block_out]
    stored_list = [stored]
    regathered = (
        lax.all_gather(ln1_gain, "grp", axis=0, tiled=True),
        lax.all_gather(ln1_shift, "grp", axis=0, tiled=True),
        lax.all_gather(qkv_weight, "grp", axis=0, tiled=True),
        lax.all_gather(qv_bias, "grp", axis=0, tiled=True),
        lax.all_gather(out_weight, "grp", axis=0, tiled=True),
        lax.all_gather(out_bias, "grp", axis=0, tiled=True),
        lax.all_gather(ln2_gain, "grp", axis=0, tiled=True),
        lax.all_gather(ln2_shift, "grp", axis=0, tiled=True),
        lax.all_gather(fc1_weight, "grp", axis=0, tiled=True),
        lax.all_gather(fc1_bias, "grp", axis=0, tiled=True),
        lax.all_gather(fc2_weight, "grp", axis=0, tiled=True),
        lax.all_gather(fc2_bias, "grp", axis=0, tiled=True),
    )
    position = 0
    input_grad, grads = backward_image(cotangent[position], stored_list[position], regathered)
    input_grads = [input_grad]
    shares = (
        lax.psum_scatter(grads[0], "grp", scatter_dimension=0, tiled=True),
        lax.psum_scatter(grads[1], "grp", scatter_dimension=0, tiled=True),
        lax.psum_scatter(grads[2], "grp", scatter_dimension=0, tiled=True),
        lax.psum_scatter(grads[3], "grp", scatter_dimension=0, tiled=True),
        lax.psum_scatter(grads[4], "grp", scatter_dimension=0, tiled=True),
        lax.psum_scatter(grads[5], "grp", scatter_dimension=0, tiled=True),
        lax.psum_scatter(grads[6], "grp", scatter_dimension=0, tiled=True),
        lax.psum_scatter(grads[7], "grp", scatter_dimension=0, tiled=True),
        lax.psum_scatter(grads[8], "grp", scatter_dimension=0, tiled=True),
        lax.psum_scatter(grads[9], "grp", scatter_dimension=0, tiled=True),
        lax.psum_scatter(grads[10], "grp", scatter_dimension=0, tiled=True),
        lax.psum_scatter(grads[11], "grp", scatter_dimension=0, tiled=True),
    )
    owned_parts = lax.psum(
        (
            shares[0],
            shares[1],
            shares[2],
            shares[3],
            shares[4],
            shares[5],
            shares[6],
            shares[7],
            shares[8],
            shares[9],
            shares[10],
            shares[11],
        ),
        "rep",
    )
    return (
        jnp.stack(block_outs),
        jnp.stack(input_grads),
        owned_parts[0],
        owned_parts[1],
        owned_parts[2],
        owned_parts[3],
        owned_parts[4],
        owned_parts[5],
        owned_parts[6],
        owned_parts[7],
        owned_parts[8],
        owned_parts[9],
        owned_parts[10],
        owned_parts[11],
    )


def solution(mesh):
    return jax.shard_map(
        on_device,
        mesh=mesh,
        in_specs=(
            P(("rep", "grp"), None, None),
            P(("rep", "grp"), None, None),
            P("grp"),
            P("grp"),
            P("grp", None),
            P("grp"),
            P("grp", None),
            P("grp"),
            P("grp"),
            P("grp"),
            P("grp", None),
            P("grp"),
            P("grp", None),
            P("grp"),
        ),
        out_specs=(
            P(("rep", "grp"), None, None),
            P(("rep", "grp"), None, None),
            P("grp"),
            P("grp"),
            P("grp", None),
            P("grp"),
            P("grp", None),
            P("grp"),
            P("grp"),
            P("grp"),
            P("grp", None),
            P("grp"),
            P("grp", None),
            P("grp"),
        ),
        check_vma=False,
    )
```

profile of v0, /device:TPU:0, one launch (start us, length us, event | category | flops | bytes accessed | tf_op | source)
XLA Modules:
  0.0 1556.5 jit_solution(15243761869660950640)
XLA Ops:
  10.2 12.8 all-gather.3
  24.2 8.0 all-gather.1
  32.3 12.8 all-gather
  45.1 17.2 %all_gather.51 = bf16[4096]{0:T(1024)(128)(2,1)S(1)} all-gather(bf16[1024]{0:T(1024)(128)(2,1)S(1)} %copy-done.30), channel_id=1, replica_groups=mesh['rep'=8,'grp'=4] {'grp'}, dimensions={0}, use_global_device_ids=true | all-gather | bytes 10240 | tf_op jit(solution)/shard_map/all_gather | solution.py:274
  62.4 8.2 all-gather.5
  70.6 17.1 %all-gather.4 = bf16[4,1,256]{2,1,0:T(2,128)(2,1)S(1)} all-gather(bf16[1,1,256]{2,1,0:T(2,128)(2,1)S(1)} %reshape.182), channel_id=1, replica_groups=mesh['rep'=8,'grp'=4] {'grp'}, dimensions={0}, use_global_device_ids=true | all-gather | bytes 2560 | tf_op jit(solution)/shard_map/all_gather | solution.py:271
  87.7 17.2 %all-gather.2 = bf16[4,1,512]{2,1,0:T(2,128)(2,1)S(1)} all-gather(bf16[1,1,512]{2,1,0:T(2,128)(2,1)S(1)} %reshape.178), channel_id=1, replica_groups=mesh['rep'=8,'grp'=4] {'grp'}, dimensions={0}, use_global_device_ids=true | all-gather | bytes 5120 | tf_op jit(solution)/shard_map/all_gather | solution.py:268
  105.7 22.4 %all-gather.12.cloned.1.call-done = bf16[1024,3072]{1,0:T(8,128)(2,1)} async-done(((bf16[256,3072]{1,0:T(8,128)(2,1)}), bf16[1024,3072]{1,0:T(8,128)(2,1)}) %all-gather.12.cloned.1.call-update) | async-done | bytes 6291472 | tf_op jit(solution)/shard_map/all_gather | solution.py:267
  128.1 6.6 fusion.90
  140.0 2.4 copy.50
  142.4 22.3 %while.28 = (s32[]{:T(128)}, bf16[4,4,577,64]{2,3,1,0:T(8,128)(2,1)}, f32[4,4,577,1]{2,1,3,0:T(4,128)S(1)}, bf16[4,4,577,64]{2,3,1,0:T(8,128)(2,1)S(1)}, bf16[4,...) while((s32[]{:T(128)}, bf16[4,4,577,64]{2,3,1,0:T(8,128)(2,1)}, ...), condition=%wide.region_5.6_spmd.clone, body=%wide.region_2.5_spmd.sunk.clone | while | flops 347575552 | bytes 27806936 | solution.py:116
  144.9 2.0 fusion.147
  150.5 2.0 fusion.147
  156.1 2.0 fusion.147
  161.7 2.0 fusion.147
  164.8 8.8 all-gather.14.cloned.1.call-done
  173.5 3.9 fusion.97
  179.3 144.3 %all-gather.16.cloned.1.call-done = bf16[1024,4096]{1,0:T(8,128)(2,1)} async-done(((bf16[256,4096]{1,0:T(8,128)(2,1)}), bf16[1024,4096]{1,0:T(8,128)(2,1)}) %all-gather.16.cloned.1.call-update) | async-done | bytes 8388624 | tf_op jit(solution)/shard_map/all_gather | solution.py:273
  323.6 12.6 multiply_convert_fusion.1
  336.1 136.7 %all-gather.18.cloned.1.call-done = bf16[4096,1024]{1,0:T(8,128)(2,1)} async-done(((bf16[1024,1024]{1,0:T(8,128)(2,1)}), bf16[4096,1024]{1,0:T(8,128)(2,1)}) %all-gather.18.cloned.1.call-update) | async-done | bytes 8388624 | tf_op jit(solution)/shard_map/all_gather | solution.py:275
  472.8 12.5 fusion.98
  485.4 5.7 multiply_reduce_fusion.1
  493.8 3.8 fusion.84
  497.6 4.8 convolution_convert_fusion
  502.4 2.4 copy.51
  504.9 37.4 %while.29 = (s32[]{:T(128)}, f32[4,4,577,64]{2,3,1,0:T(8,128)}, bf16[4,4,577,64]{2,3,1,0:T(8,128)(2,1)}, f32[4,4,577,64]{2,3,1,0:T(8,128)}, bf16[4,4,577,64]{2,3...) while((s32[]{:T(128)}, f32[4,4,577,64]{2,3,1,0:T(8,128)}, ...), condition=%wide.region_12.13_spmd.clone, body=%wide.region_10.12_spmd.sunk.clone | while | flops 864429056 | bytes 60423508 | solution.py:209
  506.4 2.3 multiply_reduce_fusion.8
  515.7 2.3 multiply_reduce_fusion.8
  525.0 2.3 multiply_reduce_fusion.8
  534.3 2.3 multiply_reduce_fusion.8
  542.2 2.1 bitcast_convert_fusion
  547.1 11.5 fusion.77
  560.3 13.3 fusion.73
  573.6 12.3 fusion.81
  586.0 208.6 %reduce-scatter.5.cloned.1.call-done = f32[256,3072]{1,0:T(8,128)} async-done(((f32[1024,3072]{1,0:T(8,128)}), f32[256,3072]{1,0:T(8,128)}) %reduce-scatter.5.cloned.1.call-update) | async-done | bytes 3145744 | tf_op jit(solution)/shard_map/reduce_scatter | solution.py:302
  794.6 283.9 %reduce-scatter.9.cloned.1.call-done = f32[256,4096]{1,0:T(8,128)} async-done(((f32[1024,4096]{1,0:T(8,128)}), f32[256,4096]{1,0:T(8,128)}) %reduce-scatter.9.cloned.1.call-update) | async-done | bytes 4194320 | tf_op jit(solution)/shard_map/reduce_scatter | solution.py:308
  1078.5 283.5 %reduce-scatter.11.cloned.1.call-done = f32[1024,1024]{1,0:T(8,128)} async-done(((f32[4096,1024]{1,0:T(8,128)}), f32[1024,1024]{1,0:T(8,128)}) %reduce-scatter.11.cloned.1.call-update) | async-done | bytes 4194320 | tf_op jit(solution)/shard_map/reduce_scatter | solution.py:310
  1362.6 10.5 all-gather.6
  1377.6 2.0 reduce_sum.185
  1379.8 10.5 fusion.67
  1390.3 16.5 %all-reduce.10 = (f32[1024]{0:T(1024)S(1)}, f32[1024]{0:T(1024)S(1)}, f32[2048]{0:T(1024)S(1)}, f32[1024]{0:T(1024)S(1)}, f32[1024]{0:T(1024)S(1)}, /*index=5*/f...) all-reduce(f32[1024]{0:T(1024)S(1)} %get-tuple-element.103, ...), channel_id=2, replica_groups=mesh['rep'=8,'grp'=4] {'grp'}, use_global_device_ids=true, to_apply=%region_16.17.clone | all-reduce | flops 12288 | bytes 98304
  1407.3 23.6 %all-reduce.8 = (f32[256]{0:T(256)}, f32[256]{0:T(256)}, f32[512]{0:T(512)}, f32[256]{0:T(256)}, f32[256]{0:T(256)}, /*index=5*/f32[256]{0:T(256)}, f32[1024]{0:T(1024)}, f32[256]{0:T(256)}) all-reduce(f32[256]{0:T(256)S(1)} %dynamic-slice.1, f32[256]{0:T(256)S(1)} %dynamic-slice.3, ...), channel_id=1, replica_groups=mesh['rep'=8,'grp'=4] {'rep'}, use_global_device_ids=true, to_apply=%region_17.18 | all-reduce | flops 3072 | bytes 24576 | tf_op jit(solution)/shard_map/psum | solution.py:313
  1430.9 5.6 fusion.80
  1436.5 9.7 fusion.79
  1446.3 92.8 %all-reduce.13.cloned.1.call-done = (f32[256,3072]{1,0:T(8,128)}, f32[256,1024]{1,0:T(8,128)}, f32[256,4096]{1,0:T(8,128)}, f32[1024,1024]{1,0:T(8,128)}) async-done(((f32[256,3072]{1,0:T(8,128)}, f32[256,1024]{1,0:T(8,128)}, f32[256,4096]{1,0:T(8,128)}, f32[1024,1024]{1,0:T(8,128)}), (f32[256,3072]{1,0:T(8,128)}, f32[256,1024]{1,0:T(8,128)}, f32[256,4096]{1,0:T(8,128)}, ...) | async-done | bytes 12582928 | tf_op jit(solution)/shard_map/psum | solution.py:313
  1539.1 4.0 copy.88
  1544.1 2.1 copy.90
  1547.8 2.0 copy.91
  (215 shorter events, 67.6 us)
Async XLA Ops:
  7.2 120.9 %all-gather.12.cloned.1.call-start = ((), (), s32[]{:S(2)}) async-start(), calls=%async_computation.4 | async-start | bytes 7864320 | tf_op jit(solution)/shard_map/all_gather | solution.py:267
  7.9 2.2 copy-start.33
  7.9 165.6 %all-gather.14.cloned.1.call-start = ((), (), s32[]{:S(2)}) async-start(), calls=%async_computation.5 | async-start | bytes 2621440 | tf_op jit(solution)/shard_map/all_gather | solution.py:269
  8.7 314.9 %all-gather.16.cloned.1.call-start = ((), (), s32[]{:S(2)}) async-start(), calls=%async_computation.6 | async-start | bytes 10485760 | tf_op jit(solution)/shard_map/all_gather | solution.py:273
  9.4 463.4 %all-gather.18.cloned.1.call-start = ((), (), s32[]{:S(2)}) async-start(), calls=%async_computation.7 | async-start | bytes 10485760 | tf_op jit(solution)/shard_map/all_gather | solution.py:275
  10.0 14.2 copy-start.34
  10.0 22.2 %copy-start.35 = (bf16[256]{0:T(256)(128)(2,1)S(1)}, bf16[256]{0:T(256)(128)(2,1)}, u32[]{:S(2)}) copy-start(bf16[256]{0:T(256)(128)(2,1)} %param.20) | copy-start | bytes 1540
  10.0 35.1 %copy-start.31 = (bf16[512]{0:T(512)(128)(2,1)S(1)}, bf16[512]{0:T(512)(128)(2,1)}, u32[]{:S(2)}) copy-start(bf16[512]{0:T(512)(128)(2,1)} %param.23) | copy-start | bytes 3076
  10.0 35.1 %copy-start.30 = (bf16[1024]{0:T(1024)(128)(2,1)S(1)}, bf16[1024]{0:T(1024)(128)(2,1)}, u32[]{:S(2)}) copy-start(bf16[1024]{0:T(1024)(128)(2,1)} %param.29) | copy-start | bytes 6148
  10.0 52.3 %copy-start.36 = (bf16[256]{0:T(256)(128)(2,1)S(1)}, bf16[256]{0:T(256)(128)(2,1)}, u32[]{:S(2)}) copy-start(bf16[256]{0:T(256)(128)(2,1)} %param.27) | copy-start | bytes 1540
  10.0 60.5 %copy-start.37 = (bf16[256]{0:T(256)(128)(2,1)S(1)}, bf16[256]{0:T(256)(128)(2,1)}, u32[]{:S(2)}) copy-start(bf16[256]{0:T(256)(128)(2,1)} %param.26) | copy-start | bytes 1540
  10.0 94.8 %copy-start.4 = (bf16[1,577,1024]{2,1,0:T(8,128)(2,1)S(1)}, bf16[1,577,1024]{2,1,0:T(8,128)(2,1)}, u32[]{:S(2)}) copy-start(bf16[1,577,1024]{2,1,0:T(8,128)(2,1)} %param.18) | copy-start | bytes 3545092
  10.1 576.0 %reduce-scatter.7.cloned.1.call-start = ((), (), s32[]{:S(2)}) async-start(), calls=%async_computation.9 | async-start | bytes 5242880 | tf_op jit(solution)/shard_map/reduce_scatter | solution.py:304
  23.1 82.5 %copy-start.8 = (bf16[4,4,577,64]{2,3,1,0:T(8,128)(2,1)}, bf16[4,4,577,64]{2,3,1,0:T(8,128)(2,1)S(1)}, u32[]{:S(2)}) copy-start(bf16[4,4,577,64]{2,3,1,0:T(8,128)(2,1)S(1)} %fusion.95) | copy-start | bytes 3545092
  32.2 102.4 %copy-start.28 = (f32[4,1,256]{2,1,0:T(1,128)}, f32[4,1,256]{2,1,0:T(1,128)S(1)}, u32[]{:S(2)}) copy-start(f32[4,1,256]{2,1,0:T(1,128)S(1)} %convert_element_type.114) | copy-start | bytes 12292
  45.1 89.5 %copy-start.24 = (f32[4,1,256]{2,1,0:T(1,128)}, f32[4,1,256]{2,1,0:T(1,128)S(1)}, u32[]{:S(2)}) copy-start(f32[4,1,256]{2,1,0:T(1,128)S(1)} %convert_element_type.113) | copy-start | bytes 12292
  105.1 29.5 %copy-start.22 = (f32[577]{0:T(1024)}, f32[577]{0:T(1024)S(1)}, u32[]{:S(2)}) copy-start(f32[577]{0:T(1024)S(1)} %broadcast_multiply_fusion.5) | copy-start | bytes 6928
  105.6 29.0 %copy-start.26 = (f32[577]{0:T(1024)}, f32[577]{0:T(1024)S(1)}, u32[]{:S(2)}) copy-start(f32[577]{0:T(1024)S(1)} %add_rsqrt_fusion.1) | copy-start | bytes 6928
  472.8 12.5 copy-start.1
  472.8 12.5 copy-start.32
  485.4 5.7 copy-start.12
  485.4 5.7 copy-start.20
  491.1 2.7 copy-start.17
  492.4 1.4 copy-start.7
  504.8 289.8 %reduce-scatter.5.cloned.1.call-start = ((), (), s32[]{:S(2)}) async-start(), calls=%async_computation.8 | async-start | bytes 15728640 | tf_op jit(solution)/shard_map/reduce_scatter | solution.py:302
  510.0 1.5 copy-start.9
  512.5 1.9 copy-start.10
  519.2 1.5 copy-start.9
  521.8 1.9 copy-start.10
  528.5 1.5 copy-start.9
  531.1 1.9 copy-start.10
  537.8 1.5 copy-start.9
  540.4 1.9 copy-start.10
  542.2 2.6 copy-start.6
  544.3 2.2 copy-start.5
  544.3 2.7 copy-start.11
  544.3 2.7 copy-start.23
  544.4 2.7 copy-start.25
  544.4 2.7 copy-start.27
  544.4 2.7 copy-start.29
  558.6 1.7 copy-start.2
  558.6 519.9 %reduce-scatter.9.cloned.1.call-start = ((), (), s32[]{:S(2)}) async-start(), calls=%async_computation.10 | async-start | bytes 20971520 | tf_op jit(solution)/shard_map/reduce_scatter | solution.py:308
  573.6 788.4 %reduce-scatter.11.cloned.1.call-start = ((), (), s32[]{:S(2)}) async-start(), calls=%async_computation.11 | async-start | bytes 20971520 | tf_op jit(solution)/shard_map/reduce_scatter | solution.py:310
  585.9 953.1 %all-reduce.13.cloned.1.call-start = ((), (), s32[]{:S(2)}) async-start(), calls=%async_computation.12 | async-start | bytes 25165824 | tf_op jit(solution)/shard_map/psum | solution.py:313
  1361.9 11.1 copy-start.39
  1539.1 4.0 copy-start.21
  1539.1 5.0 copy-start.14
  1544.1 3.7 copy-start.13
  (16 other events, 19.2 us)
Sparse Core Ops, SparseCore 0:
  9.6 118.4 all-gather.11
  129.6 43.8 all-gather.13
  175.1 148.4 all-gather.15
  325.0 147.7 all-gather.17
  505.0 74.9 reduce-scatter.6
  582.2 212.3 reduce-scatter.4
  797.0 281.4 reduce-scatter.8
  1080.8 281.0 reduce-scatter.10
  1365.9 173.1 all-reduce.12
where the time goes:
time: 1570 us; the launch traced here: 1560 us
  waiting for transfers between devices  1180 us (75%)
  matrix products  151 us (10%)
  blocking collectives  144 us (9%)
  local copies, waits for them, and re-layouts  35.9 us (2%)
  other arithmetic  24.6 us (2%)
  between operations  16.5 us (1%)
    reduce_scatter x1, waiting for transfers between devices, on_device(): lax.psum_scatter(grads[8], 'grp', scatter_dimension=0, tiled=True)  284 us
    reduce_scatter x1, waiting for transfers between devices, on_device(): lax.psum_scatter(grads[10], 'grp', scatter_dimension=0, tiled=True)  283 us
    reduce_scatter x1, waiting for transfers between devices, on_device(): lax.psum_scatter(grads[2], 'grp', scatter_dimension=0, tiled=True)  209 us
    all_gather x1, waiting for transfers between devices, on_device(): lax.all_gather(fc1_weight, 'grp', axis=0, tiled=True)  144 us
    all_gather x1, waiting for transfers between devices, on_device(): lax.all_gather(fc2_weight, 'grp', axis=0, tiled=True)  137 us
    psum x1, waiting for transfers between devices, on_device(): lax.psum((shares[0], shares[1], shares[2], shares[3], shares[4], shares[5...  92.8 us
  transfers between devices with their start and end apart: 9, of which 8 were waited for; matrix products, arithmetic and copies ran while one was open for 10% of the time, Pallas kernels for 0%

commit v1 on v0

--- a/solution.py
+++ b/solution.py
@@ -8,6 +8,27 @@
 HD = 64
 root_half = 0.7071067811865476
 inv_root_tau = 0.3989422804014327
+
+
+def gather_around(x, axis, dim):
+    peers, here, width = (lax.axis_size(axis), lax.axis_index(axis), x.shape[dim])
+    right = [(i, (i + 1) % peers) for i in range(peers)]
+    behind = [(i, (i - 1) % peers) for i in range(peers)]
+    whole = jnp.zeros((*x.shape[:dim], peers * width, *x.shape[dim + 1 :]), x.dtype)
+    whole = lax.dynamic_update_slice_in_dim(whole, x, here * width, axis=dim)
+    from_left = from_right = x
+    half = peers // 2
+    for step in range(1, half + 1):
+        from_left = lax.ppermute(from_left, axis, right)
+        whole = lax.dynamic_update_slice_in_dim(
+            whole, from_left, (here - step) % peers * width, axis=dim
+        )
+        if step < peers - half:
+            from_right = lax.ppermute(from_right, axis, behind)
+            whole = lax.dynamic_update_slice_in_dim(
+                whole, from_right, (here + step) % peers * width, axis=dim
+            )
+    return whole
 
 
 def norm_forward(values, gain_vec, shift_vec):
@@ -272,7 +293,7 @@
         lax.all_gather(ln2_shift, "grp", axis=0, tiled=True),
         lax.all_gather(fc1_weight, "grp", axis=0, tiled=True),
         lax.all_gather(fc1_bias, "grp", axis=0, tiled=True),
-        lax.all_gather(fc2_weight, "grp", axis=0, tiled=True),
+        gather_around(fc2_weight, "grp", 0),
         lax.all_gather(fc2_bias, "grp", axis=0, tiled=True),
     )
     position = 0

time: 1570 us -> 1660 us (1.057)
  blocking collectives: 144 us -> 182 us
  waiting for transfers between devices: 1180 us -> 1210 us
  local copies, waits for them, and re-layouts: 35.9 us -> 54.9 us
    reduce_scatter x1, waiting for transfers between devices: 209 us -> 289 us  [on_device(): lax.psum_scatter(grads[2], 'grp', scatter_dimension=0, tiled=True)]
    psum x1, waiting for transfers between devices: 92.8 us -> 38 us  [on_device(): lax.psum((shares[0], shares[1], shares[2], shares[3], shares[4], shares[5...]
    all_gather x1, blocking collectives: 10.5 us -> 49.1 us  [on_device(): lax.all_gather(fc2_bias, 'grp', axis=0, tiled=True)]
  transfers between devices with their start and end apart: 9 -> 12, of which waited for: 8 -> 8; matrix products, arithmetic and copies ran while one was open for 10% -> 11% of each run, Pallas kernels for 0% -> 0%
where the time goes in v1:
time: 1660 us; the launch traced here: 1650 us
  waiting for transfers between devices  1210 us (73%)
  blocking collectives  182 us (11%)
  matrix products  152 us (9%)
  local copies, waits for them, and re-layouts  54.9 us (3%)
  other arithmetic  27 us (2%)
  between operations  16.6 us (1%)
    reduce_scatter x1, waiting for transfers between devices, on_device(): lax.psum_scatter(grads[2], 'grp', scatter_dimension=0, tiled=True)  289 us
    reduce_scatter x1, waiting for transfers between devices, on_device(): lax.psum_scatter(grads[10], 'grp', scatter_dimension=0, tiled=True)  283 us
    reduce_scatter x1, waiting for transfers between devices, on_device(): lax.psum_scatter(grads[8], 'grp', scatter_dimension=0, tiled=True)  283 us
    all_gather x1, waiting for transfers between devices, on_device(): lax.all_gather(fc1_weight, 'grp', axis=0, tiled=True)  144 us
    all_gather x1, waiting for transfers between devices, on_device(): lax.all_gather(fc2_weight, 'grp', axis=0, tiled=True)  137 us
    all_gather x1, blocking collectives, on_device(): lax.all_gather(fc2_bias, 'grp', axis=0, tiled=True)  49.1 us
    psum x1, waiting for transfers between devices, on_device(): lax.psum((shares[0], shares[1], shares[2], shares[3], shares[4], shares[5...  38 us
  transfers between devices with their start and end apart: 12, of which 8 were waited for; matrix products, arithmetic and copies ran while one was open for 11% of the time, Pallas kernels for 0%

profile of v1, /device:TPU:0, one launch (start us, length us, event | category | flops | bytes accessed | tf_op | source)
XLA Modules:
  0.0 1646.6 jit_solution(7917604791493379764)
XLA Ops:
  10.2 12.8 all-gather
  23.0 8.0 all-gather.1
  33.4 11.9 all-gather.3
  45.3 8.2 all-gather.4
  53.5 18.6 %all_gather.50 = bf16[4096]{0:T(1024)(128)(2,1)S(1)} all-gather(bf16[1024]{0:T(1024)(128)(2,1)S(1)} %copy-done.31), channel_id=1, replica_groups=mesh['rep'=8,'grp'=4] {'grp'}, dimensions={0}, use_global_device_ids=true | all-gather | bytes 10240 | tf_op jit(solution)/shard_map/all_gather | solution.py:295
  72.1 15.6 all-gather.5
  87.7 17.1 %all-gather.2 = bf16[4,1,512]{2,1,0:T(2,128)(2,1)S(1)} all-gather(bf16[1,1,512]{2,1,0:T(2,128)(2,1)S(1)} %reshape.178), channel_id=1, replica_groups=mesh['rep'=8,'grp'=4] {'grp'}, dimensions={0}, use_global_device_ids=true | all-gather | bytes 5120 | tf_op jit(solution)/shard_map/all_gather | solution.py:289
  105.6 22.6 %all-gather.12.cloned.1.call-done = bf16[1024,3072]{1,0:T(8,128)(2,1)} async-done(((bf16[256,3072]{1,0:T(8,128)(2,1)}), bf16[1024,3072]{1,0:T(8,128)(2,1)}) %all-gather.12.cloned.1.call-update) | async-done | bytes 6291472 | tf_op jit(solution)/shard_map/all_gather | solution.py:288
  128.1 6.6 fusion.90
  142.5 22.3 %while.28 = (s32[]{:T(128)}, bf16[4,4,577,64]{2,3,1,0:T(8,128)(2,1)}, f32[4,4,577,1]{2,1,3,0:T(4,128)S(1)}, bf16[4,4,577,64]{2,3,1,0:T(8,128)(2,1)S(1)}, bf16[4,...) while((s32[]{:T(128)}, bf16[4,4,577,64]{2,3,1,0:T(8,128)(2,1)}, ...), condition=%wide.region_5.6_spmd.clone, body=%wide.region_2.5_spmd.sunk.clone | while | flops 347575552 | bytes 27806928 | solution.py:137
  150.5 2.0 fusion.147
  164.8 8.7 all-gather.14.cloned.1.call-done
  173.5 3.9 fusion.97
  179.2 144.3 %all-gather.16.cloned.1.call-done = bf16[1024,4096]{1,0:T(8,128)(2,1)} async-done(((bf16[256,4096]{1,0:T(8,128)(2,1)}), bf16[1024,4096]{1,0:T(8,128)(2,1)}) %all-gather.16.cloned.1.call-update) | async-done | bytes 8388624 | tf_op jit(solution)/shard_map/all_gather | solution.py:294
  323.6 12.5 multiply_convert_fusion.1
  336.1 136.7 %all-gather.18.cloned.1.call-done = bf16[4096,1024]{1,0:T(8,128)(2,1)} async-done(((bf16[1024,1024]{1,0:T(8,128)(2,1)}), bf16[4096,1024]{1,0:T(8,128)(2,1)}) %all-gather.18.cloned.1.call-update) | async-done | bytes 8388624 | tf_op jit(solution)/shard_map/all_gather | solution.py:314
  472.8 13.1 fusion.98
  486.0 5.7 multiply_reduce_fusion.1
  494.4 3.8 fusion.84
  498.2 4.8 convolution_convert_fusion
  503.0 2.4 copy.51
  505.5 41.9 %while.29 = (s32[]{:T(128)}, f32[4,4,577,64]{2,3,1,0:T(8,128)}, bf16[4,4,577,64]{2,3,1,0:T(8,128)(2,1)}, f32[4,4,577,64]{2,3,1,0:T(8,128)}, bf16[4,4,577,64]{2,3...) while((s32[]{:T(128)}, f32[4,4,577,64]{2,3,1,0:T(8,128)}, ...), condition=%wide.region_12.13_spmd.clone, body=%wide.region_10.12_spmd.sunk.clone | while | flops 864429056 | bytes 60423500 | solution.py:230
  507.0 2.3 multiply_reduce_fusion.8
  517.4 2.3 multiply_reduce_fusion.8
  527.9 2.3 multiply_reduce_fusion.8
  538.3 2.3 multiply_reduce_fusion.8
  549.4 2.4 bitcast_convert_fusion
  553.0 11.6 fusion.77
  566.2 13.3 fusion.73
  579.6 12.8 fusion.81
  592.6 3.8 collective-permute-start.1
  596.4 288.7 %reduce-scatter.5.cloned.1.call-done = f32[256,3072]{1,0:T(8,128)} async-done(((f32[1024,3072]{1,0:T(8,128)}), f32[256,3072]{1,0:T(8,128)}) %reduce-scatter.5.cloned.1.call-update) | async-done | bytes 3145744 | tf_op jit(solution)/shard_map/reduce_scatter | solution.py:323
  885.1 283.4 %reduce-scatter.9.cloned.1.call-done = f32[256,4096]{1,0:T(8,128)} async-done(((f32[1024,4096]{1,0:T(8,128)}), f32[256,4096]{1,0:T(8,128)}) %reduce-scatter.9.cloned.1.call-update) | async-done | bytes 4194320 | tf_op jit(solution)/shard_map/reduce_scatter | solution.py:329
  1168.5 283.5 %reduce-scatter.11.cloned.1.call-done = f32[1024,1024]{1,0:T(8,128)} async-done(((f32[4096,1024]{1,0:T(8,128)}), f32[1024,1024]{1,0:T(8,128)}) %reduce-scatter.11.cloned.1.call-update) | async-done | bytes 4194320 | tf_op jit(solution)/shard_map/reduce_scatter | solution.py:331
  1455.1 49.1 %all-gather.6 = bf16[4,1,256]{2,1,0:T(2,128)(2,1)S(1)} all-gather(bf16[1,1,256]{2,1,0:T(2,128)(2,1)S(1)} %reshape.186), channel_id=1, replica_groups=mesh['rep'=8,'grp'=4] {'grp'}, dimensions={0}, use_global_device_ids=true | all-gather | bytes 2560 | tf_op jit(solution)/shard_map/all_gather | solution.py:297
  1504.2 4.3 broadcast_in_dim.22
  1510.0 3.1 constant_dynamic-update-slice_fusion.2
  1513.1 3.1 constant_dynamic-update-slice_fusion.1
  1516.3 3.1 constant_dynamic-update-slice_fusion
  1521.4 2.4 reduce_sum.187
  1523.9 10.3 fusion.67
  1534.2 17.8 %all-reduce.10 = (f32[1024]{0:T(1024)S(1)}, f32[1024]{0:T(1024)S(1)}, f32[2048]{0:T(1024)S(1)}, f32[1024]{0:T(1024)S(1)}, f32[1024]{0:T(1024)S(1)}, /*index=5*/f...) all-reduce(f32[1024]{0:T(1024)S(1)} %get-tuple-element.103, ...), channel_id=2, replica_groups=mesh['rep'=8,'grp'=4] {'grp'}, use_global_device_ids=true, to_apply=%region_16.17.clone | all-reduce | flops 12288 | bytes 98304
  1552.4 23.4 %all-reduce.8 = (f32[256]{0:T(256)}, f32[256]{0:T(256)}, f32[512]{0:T(512)}, f32[256]{0:T(256)}, f32[256]{0:T(256)}, /*index=5*/f32[256]{0:T(256)}, f32[1024]{0:T(1024)}, f32[256]{0:T(256)}) all-reduce(f32[256]{0:T(256)S(1)} %dynamic-slice.1, f32[256]{0:T(256)S(1)} %dynamic-slice.3, ...), channel_id=1, replica_groups=mesh['rep'=8,'grp'=4] {'rep'}, use_global_device_ids=true, to_apply=%region_17.18 | all-reduce | flops 3072 | bytes 24576 | tf_op jit(solution)/shard_map/psum | solution.py:334
  1575.8 5.4 fusion.80
  1581.2 9.9 fusion.79
  1591.1 38.0 %all-reduce.13.cloned.1.call-done = (f32[256,3072]{1,0:T(8,128)}, f32[256,1024]{1,0:T(8,128)}, f32[256,4096]{1,0:T(8,128)}, f32[1024,1024]{1,0:T(8,128)}) async-done(((f32[256,3072]{1,0:T(8,128)}, f32[256,1024]{1,0:T(8,128)}, f32[256,4096]{1,0:T(8,128)}, f32[1024,1024]{1,0:T(8,128)}), (f32[256,3072]{1,0:T(8,128)}, f32[256,1024]{1,0:T(8,128)}, f32[256,4096]{1,0:T(8,128)}, ...) | async-done | bytes 12582928 | tf_op jit(solution)/shard_map/psum | solution.py:334
  1629.1 4.0 copy.90
  1634.2 2.1 copy.92
  (228 shorter events, 85.4 us)
Async XLA Ops:
  7.2 120.9 %all-gather.12.cloned.1.call-start = ((), (), s32[]{:S(2)}) async-start(), calls=%async_computation.4 | async-start | bytes 7864320 | tf_op jit(solution)/shard_map/all_gather | solution.py:288
  7.9 2.2 copy-start.34
  7.9 15.0 copy-start.35
  7.9 23.1 %copy-start.32 = (bf16[512]{0:T(512)(128)(2,1)S(1)}, bf16[512]{0:T(512)(128)(2,1)}, u32[]{:S(2)}) copy-start(bf16[512]{0:T(512)(128)(2,1)} %param.23) | copy-start | bytes 3076
  7.9 165.6 %all-gather.14.cloned.1.call-start = ((), (), s32[]{:S(2)}) async-start(), calls=%async_computation.5 | async-start | bytes 2621440 | tf_op jit(solution)/shard_map/all_gather | solution.py:290
  8.7 314.9 %all-gather.16.cloned.1.call-start = ((), (), s32[]{:S(2)}) async-start(), calls=%async_computation.6 | async-start | bytes 10485760 | tf_op jit(solution)/shard_map/all_gather | solution.py:294
  9.4 463.4 %all-gather.18.cloned.1.call-start = ((), (), s32[]{:S(2)}) async-start(), calls=%async_computation.7 | async-start | bytes 10485760 | tf_op jit(solution)/shard_map/all_gather | solution.py:314
  10.0 23.4 %copy-start.36 = (bf16[256]{0:T(256)(128)(2,1)S(1)}, bf16[256]{0:T(256)(128)(2,1)}, u32[]{:S(2)}) copy-start(bf16[256]{0:T(256)(128)(2,1)} %param.25) | copy-start | bytes 1540
  10.0 35.3 %copy-start.37 = (bf16[256]{0:T(256)(128)(2,1)S(1)}, bf16[256]{0:T(256)(128)(2,1)}, u32[]{:S(2)}) copy-start(bf16[256]{0:T(256)(128)(2,1)} %param.26) | copy-start | bytes 1540
  10.0 43.5 %copy-start.31 = (bf16[1024]{0:T(1024)(128)(2,1)S(1)}, bf16[1024]{0:T(1024)(128)(2,1)}, u32[]{:S(2)}) copy-start(bf16[1024]{0:T(1024)(128)(2,1)} %param.29) | copy-start | bytes 6148
  10.0 62.0 %copy-start.38 = (bf16[256]{0:T(256)(128)(2,1)S(1)}, bf16[256]{0:T(256)(128)(2,1)}, u32[]{:S(2)}) copy-start(bf16[256]{0:T(256)(128)(2,1)} %param.27) | copy-start | bytes 1540
  10.0 94.7 %copy-start.4 = (bf16[1,577,1024]{2,1,0:T(8,128)(2,1)S(1)}, bf16[1,577,1024]{2,1,0:T(8,128)(2,1)}, u32[]{:S(2)}) copy-start(bf16[1,577,1024]{2,1,0:T(8,128)(2,1)} %param.18) | copy-start | bytes 3545092
  10.1 586.3 %reduce-scatter.7.cloned.1.call-start = ((), (), s32[]{:S(2)}) async-start(), calls=%async_computation.9 | async-start | bytes 5242880 | tf_op jit(solution)/shard_map/reduce_scatter | solution.py:325
  23.0 105.2 %copy-start.24 = (f32[4,1,256]{2,1,0:T(1,128)}, f32[4,1,256]{2,1,0:T(1,128)S(1)}, u32[]{:S(2)}) copy-start(f32[4,1,256]{2,1,0:T(1,128)S(1)} %convert_element_type.113) | copy-start | bytes 12292
  31.0 97.1 %copy-start.29 = (f32[4,1,256]{2,1,0:T(1,128)}, f32[4,1,256]{2,1,0:T(1,128)S(1)}, u32[]{:S(2)}) copy-start(f32[4,1,256]{2,1,0:T(1,128)S(1)} %convert_element_type.114) | copy-start | bytes 12292
  105.0 29.6 %copy-start.22 = (f32[577]{0:T(1024)}, f32[577]{0:T(1024)S(1)}, u32[]{:S(2)}) copy-start(f32[577]{0:T(1024)S(1)} %broadcast_multiply_fusion.5) | copy-start | bytes 6928
  105.5 29.2 %copy-start.26 = (f32[577]{0:T(1024)}, f32[577]{0:T(1024)S(1)}, u32[]{:S(2)}) copy-start(f32[577]{0:T(1024)S(1)} %add_rsqrt_fusion.1) | copy-start | bytes 6928
  472.8 13.1 copy-start.1
  472.8 13.1 copy-start.33
  486.0 5.7 copy-start.12
  486.0 5.7 copy-start.20
  491.7 2.7 copy-start.17
  493.0 1.4 copy-start.6
  505.4 379.7 %reduce-scatter.5.cloned.1.call-start = ((), (), s32[]{:S(2)}) async-start(), calls=%async_computation.8 | async-start | bytes 15728640 | tf_op jit(solution)/shard_map/reduce_scatter | solution.py:323
  510.6 1.5 copy-start.9
  521.0 1.5 copy-start.9
  531.5 1.5 copy-start.9
  541.9 1.5 copy-start.9
  549.3 2.5 copy-start.18
  549.3 3.7 copy-start.5
  549.3 3.7 copy-start.11
  549.3 3.7 copy-start.23
  549.3 3.6 copy-start.25
  549.3 3.6 copy-start.27
  549.4 3.6 copy-start.30
  564.5 1.7 copy-start.2
  564.6 603.9 %reduce-scatter.9.cloned.1.call-start = ((), (), s32[]{:S(2)}) async-start(), calls=%async_computation.10 | async-start | bytes 20971520 | tf_op jit(solution)/shard_map/reduce_scatter | solution.py:329
  579.5 872.4 %reduce-scatter.11.cloned.1.call-start = ((), (), s32[]{:S(2)}) async-start(), calls=%async_computation.11 | async-start | bytes 20971520 | tf_op jit(solution)/shard_map/reduce_scatter | solution.py:331
  592.4 1036.7 %all-reduce.13.cloned.1.call-start = ((), (), s32[]{:S(2)}) async-start(), calls=%async_computation.12 | async-start | bytes 25165824 | tf_op jit(solution)/shard_map/psum | solution.py:334
  592.5 859.5 %collective-permute-start = (bf16[1024,1024]{1,0:T(8,128)(2,1)}, bf16[1024,1024]{1,0:T(8,128)(2,1)}, u32[]{:S(2)}, u32[]{:S(2)}) collective-permute-start(bf16[1024,1024]{1,0:T(8,128)(2,1)} %param.30), channel_id=1, source_target_pairs={{0,1},{1,2},{2,3},{3,0},{4,5},{5,6},{6,7},{7,4},{8,9},{9,10},{10,1... | collective-permute-start | bytes 6291464 | tf_op jit(solution)/shard_map/ppermute | solution.py:22
  592.6 920.6 %collective-permute-start.1 = (bf16[1024,1024]{1,0:T(8,128)(2,1)}, bf16[1024,1024]{1,0:T(8,128)(2,1)}, u32[]{:S(2)}, u32[]{:S(2)}) collective-permute-start(bf16[1024,1024]{1,0:T(8,128)(2,1)} %param.30), channel_id=1, source_target_pairs={{0,3},{1,0},{2,1},{3,2},{4,7},{5,4},{6,5},{7,6},{8,11},{9,8},{10,9... | collective-permute-start | bytes 6291464 | tf_op jit(solution)/shard_map/ppermute | solution.py:27
  1451.9 3.2 copy-start.39
  1452.0 64.3 %collective-permute-start.2 = (bf16[1024,1024]{1,0:T(8,128)(2,1)}, bf16[1024,1024]{1,0:T(8,128)(2,1)}, u32[]{:S(2)}, u32[]{:S(2)}) collective-permute-start(bf16[1024,1024]{1,0:T(8,128)(2,1)} %collective-permute-done), channel_id=1, source_target_pairs={{0,1},{1,2},{2,3},{3,0},{4,5},{5,6},{6,7},{7,4},{8,9},{9,10},{10,1... | collective-permute-start | bytes 6291464 | tf_op jit(solution)/shard_map/ppermute | solution.py:22
  1504.2 4.3 copy-start.7
  1523.8 10.3 copy-start.28
  1629.1 4.0 copy-start.21
  1629.1 5.0 copy-start.14
  1634.2 3.7 copy-start.13
  (20 other events, 23.5 us)
Sparse Core Ops, SparseCore 0:
  9.6 118.4 all-gather.11
  129.7 43.7 all-gather.13
  175.1 148.4 all-gather.15
  325.0 147.7 all-gather.17
  505.6 74.9 reduce-scatter.6
  582.8 302.2 reduce-scatter.4
  887.5 280.9 reduce-scatter.8
  1170.8 281.0 reduce-scatter.10
  1455.9 173.1 all-reduce.12
